TPU v7x, 32 devices: a whole 2x2x4 slice. The times are simulated.
32 devices in a mesh: dp: 2 (over x), expert: 16 (over z, y, core).
Axes of the slice: x: 2, y: 2, z: 4, core: 2. Of those that a mesh axis runs over, the one named last changes fastest.
Arguments:
- tokens: bfloat16 [4096, 1024], P(('dp', 'expert')), may hold values from -6 to 6
- cotangent: bfloat16 [4096, 1024], P(('dp', 'expert')), may hold values from -6 to 6
- expert_ids: int32 [4096, 6], P(('dp', 'expert')), may hold values from 0 to 15, all different within a row; in each aligned block of 128 rows (0 to 127, 128 to 255, ...) at most 60 rows name the same one
- gate_weights: float32 [4096, 6], P(('dp', 'expert')), may hold values from 0.05 to 0.3
- partner: int32 [16], replicated, may hold values from 0 to 15, as said below
- weights: bfloat16 [16, 1024, 3, 384], P('expert', 'dp'), may hold values from -0.3125 to 0.3125
- first_moment: bfloat16 [16, 1024, 3, 384], P('expert', 'dp'), may hold values from -6 to 6
- second_moment: bfloat16 [16, 1024, 3, 384], P('expert', 'dp'), may hold values from 0.099609375 to 4
Outputs:
- mixed: bfloat16 [4096, 1024], P(('dp', 'expert'))
- token_grad: bfloat16 [4096, 1024], P(('dp', 'expert'))
- new_weights: bfloat16 [16, 1024, 3, 384], P('expert', 'dp')
- new_first: bfloat16 [16, 1024, 3, 384], P('expert', 'dp')
- new_second: bfloat16 [16, 1024, 3, 384], P('expert', 'dp')
Inputs may be any that keep to these rules, and one draw needn't show every extreme that they name: `expert_ids`: each row names 6 different experts. Among the 128 tokens of one device (aligned blocks of rows), no expert is named by more than 60 tokens, and in every draw some block names some expert exactly 60 times. partner[partner[h]] = h and partner[h] != h for every h.
All inputs are finite; a program needn't handle non-finite values.
Results may differ from a plain program's by a relative error of at most 0.024.
Values may be sent and summed in bfloat16 or wider, within the bound.
A program may use at most 64 MiB of HBM per device.

v0:
```python
import jax
import jax.numpy as jnp
from jax import lax
from jax.sharding import PartitionSpec as P

beta_one = 0.9
beta_two = 0.95
learn_rate = 0.01
decay_rate = 0.1
eps_adam = 1e-08
step_count = 100


def send_rows(parts):
    return (lax.all_to_all(parts[0], "expert", split_axis=0, concat_axis=0, tiled=True),)


def send_back(parts):
    return (lax.all_to_all(parts[0], "expert", split_axis=0, concat_axis=0, tiled=True),)


def shards_by_slot(
    tokens, cotangent, expert_ids, gate_weights, partner, weights, first_moment, second_moment
):
    experts_here = lax.axis_size("expert")
    tok_dev, model_width = tokens.shape
    top_count = expert_ids.shape[1]
    hidden_width = weights.shape[3]
    capacity = min(tok_dev, max(2, 5 * tok_dev * top_count // (4 * experts_here)))
    item_total = tok_dev * top_count
    slot_total = experts_here * capacity
    flat_ids = expert_ids.reshape(item_total)
    onehot = (flat_ids[:, None] == jnp.arange(experts_here, dtype=jnp.int32)[None, :]).astype(
        jnp.int32
    )
    before = jnp.cumsum(onehot, axis=0) - onehot
    slot_of = jnp.sum(before * onehot, axis=1)
    position = flat_ids * capacity + slot_of
    source = (
        jnp.full((slot_total,), item_total, jnp.int32)
        .at[position]
        .set(jnp.arange(item_total, dtype=jnp.int32))
    )
    token_of = source // top_count
    zero_row = jnp.zeros((1, model_width), jnp.bfloat16)
    x_send = jnp.concatenate([tokens, zero_row], axis=0)[token_of].reshape(
        experts_here, capacity, model_width
    )
    gate_flat = gate_weights.reshape(item_total)
    gate_pad = jnp.concatenate([gate_flat, jnp.zeros((1,), jnp.float32)])
    cot_rows = jnp.concatenate([cotangent, zero_row], axis=0)[token_of].astype(jnp.float32)
    dy_send = (
        (gate_pad[source][:, None] * cot_rows)
        .astype(jnp.bfloat16)
        .reshape(experts_here, capacity, model_width)
    )
    gathered = lax.all_gather(weights, "dp", axis=1, tiled=True)[0]
    gate_up = gathered[:, 0:2, :].reshape(model_width, 2 * hidden_width)
    down_proj = gathered[:, 2, :]
    block_shape = (experts_here, capacity, model_width)
    (x_recv,) = send_rows((x_send,))
    forward_x_rows = x_recv.reshape(slot_total, model_width)
    both_proj = jnp.dot(forward_x_rows, gate_up, preferred_element_type=jnp.float32)
    pre_act = both_proj[:, :hidden_width]
    lin_act = both_proj[:, hidden_width:]
    sigmoid_pre = jax.nn.sigmoid(pre_act)
    silu_pre = pre_act * sigmoid_pre
    forward_hidden = (silu_pre * lin_act).astype(jnp.bfloat16)
    out_rows = jnp.dot(forward_hidden, down_proj.T, preferred_element_type=jnp.float32).astype(
        jnp.bfloat16
    )
    x_rows, saved, hidden, out_rows = (
        forward_x_rows,
        (pre_act, lin_act, sigmoid_pre, silu_pre),
        forward_hidden,
        out_rows,
    )
    (out_back,) = send_back((out_rows.reshape(block_shape),))
    (dy_recv,) = send_rows((dy_send,))
    pre_act, lin_act, sigmoid_pre, silu_pre = saved
    backward_dy_rows = dy_recv.reshape(slot_total, model_width)
    hidden_grad = jnp.dot(backward_dy_rows, down_proj, preferred_element_type=jnp.float32)
    pre_grad = (hidden_grad * lin_act * sigmoid_pre * (1.0 + pre_act * (1.0 - sigmoid_pre))).astype(
        jnp.bfloat16
    )
    lin_grad = (hidden_grad * silu_pre).astype(jnp.bfloat16)
    backward_both_grad = jnp.concatenate([pre_grad, lin_grad], axis=1)
    item_grad = jnp.dot(backward_both_grad, gate_up.T, preferred_element_type=jnp.float32).astype(
        jnp.bfloat16
    )
    dy_rows, both_grad, item_grad = (backward_dy_rows, backward_both_grad, item_grad)
    (grad_back,) = send_back((item_grad.reshape(block_shape),))
    out_items = (
        out_back.reshape(slot_total, model_width)[position].astype(jnp.float32) * gate_flat[:, None]
    )
    mixed = jnp.sum(out_items.reshape(tok_dev, top_count, model_width), axis=1).astype(jnp.bfloat16)
    grad_items = grad_back.reshape(slot_total, model_width)[position].astype(jnp.float32)
    token_grad = jnp.sum(grad_items.reshape(tok_dev, top_count, model_width), axis=1).astype(
        jnp.bfloat16
    )
    count = lax.axis_size("dp") * weights.shape[1]
    proj_grad = jnp.dot(x_rows.T, both_grad, preferred_element_type=jnp.float32)
    down_grad = jnp.dot(dy_rows.T, hidden, preferred_element_type=jnp.float32)
    grad_sum = lax.psum_scatter(
        jnp.concatenate(
            [proj_grad.reshape(count, 2, hidden_width), down_grad.reshape(count, 1, hidden_width)],
            axis=1,
        ).astype(jnp.bfloat16),
        "dp",
        scatter_dimension=0,
        tiled=True,
    ).astype(jnp.float32)
    w_old = weights[0].astype(jnp.float32)
    m_old = first_moment[0].astype(jnp.float32)
    v_old = second_moment[0].astype(jnp.float32)
    m_new = beta_one * m_old + (1.0 - beta_one) * grad_sum
    v_new = beta_two * v_old + (1.0 - beta_two) * grad_sum * grad_sum
    m_hat = m_new / (1.0 - beta_one**step_count)
    v_hat = v_new / (1.0 - beta_two**step_count)
    w_new = w_old - learn_rate * (m_hat / (jnp.sqrt(v_hat) + eps_adam) + decay_rate * w_old)
    pieces = (
        w_new.astype(jnp.bfloat16).reshape(experts_here, -1),
        m_new.astype(jnp.bfloat16).reshape(experts_here, -1),
        v_new.astype(jnp.bfloat16).reshape(experts_here, -1),
    )
    spread = (
        lax.all_to_all(pieces[0], "expert", split_axis=0, concat_axis=0, tiled=True),
        lax.all_to_all(pieces[1], "expert", split_axis=0, concat_axis=0, tiled=True),
        lax.all_to_all(pieces[2], "expert", split_axis=0, concat_axis=0, tiled=True),
    )
    ordered = (spread[0][partner], spread[1][partner], spread[2][partner])
    homed = (
        lax.all_to_all(ordered[0], "expert", split_axis=0, concat_axis=0, tiled=True),
        lax.all_to_all(ordered[1], "expert", split_axis=0, concat_axis=0, tiled=True),
        lax.all_to_all(ordered[2], "expert", split_axis=0, concat_axis=0, tiled=True),
    )
    new_weights = homed[0].reshape(weights.shape)
    new_first = homed[1].reshape(weights.shape)
    new_second = homed[2].reshape(weights.shape)
    return (mixed, token_grad, new_weights, new_first, new_second)


def adam(w_old, m_old, v_old, grad_sum):
    m_new = beta_one * m_old + (1.0 - beta_one) * grad_sum
    v_new = beta_two * v_old + (1.0 - beta_two) * grad_sum * grad_sum
    m_hat = m_new / (1.0 - beta_one**step_count)
    v_hat = v_new / (1.0 - beta_two**step_count)
    w_new = w_old - learn_rate * (m_hat / (jnp.sqrt(v_hat) + eps_adam) + decay_rate * w_old)
    return (w_new, m_new, v_new)


def shards_dense(
    tokens, cotangent, expert_ids, gate_weights, partner, weights, first_moment, second_moment
):
    experts_here = lax.axis_size("expert")
    me = lax.axis_index("expert")
    tok_dev, model_width = tokens.shape
    own_rows, hidden_width = (weights.shape[1], weights.shape[3])
    width = 3 * hidden_width
    f32, bf16 = (jnp.float32, jnp.bfloat16)
    hits = expert_ids[:, :, None] == jnp.arange(experts_here, dtype=jnp.int32)[None, None, :]
    gate_table = jnp.sum(jnp.where(hits, gate_weights[:, :, None], 0.0), axis=1).T
    w_flat = weights[0].reshape(own_rows, width)
    gathered = lax.all_gather(w_flat, "dp", axis=0, tiled=True)
    x_rows = lax.all_gather(tokens, "expert", axis=0, tiled=True)
    cot_rows = lax.all_gather(cotangent, "expert", axis=0, tiled=True)
    gate_all = lax.all_gather(gate_table, "expert", axis=0)
    gate = lax.dynamic_index_in_dim(gate_all, me, 1, keepdims=False)
    gate = gate.reshape(experts_here * tok_dev, 1)
    gate_up = gathered[:, : 2 * hidden_width]
    down_proj = gathered[:, 2 * hidden_width :]
    both_proj = jnp.dot(x_rows, gate_up, preferred_element_type=f32)
    pre_act = both_proj[:, :hidden_width]
    lin_act = both_proj[:, hidden_width:]
    sigmoid_pre = jax.nn.sigmoid(pre_act)
    silu_pre = pre_act * sigmoid_pre
    hidden = (silu_pre * lin_act).astype(bf16)
    out_rows = jnp.dot(hidden, down_proj.T, preferred_element_type=f32)
    mixed = lax.psum_scatter(
        (gate * out_rows).astype(bf16), "expert", scatter_dimension=0, tiled=True
    )
    dy_rows = (gate * cot_rows.astype(f32)).astype(bf16)
    hidden_grad = jnp.dot(dy_rows, down_proj, preferred_element_type=f32)
    pre_grad = hidden_grad * lin_act * sigmoid_pre * (1.0 + pre_act * (1.0 - sigmoid_pre))
    lin_grad = hidden_grad * silu_pre
    both_grad = jnp.concatenate([pre_grad.astype(bf16), lin_grad.astype(bf16)], axis=1)
    proj_grad = jnp.dot(x_rows.T, both_grad, preferred_element_type=f32)
    down_grad = jnp.dot(dy_rows.T, hidden, preferred_element_type=f32)
    partial = jnp.concatenate([proj_grad.astype(bf16), down_grad.astype(bf16)], axis=1)
    grad_sum = lax.psum_scatter(partial, "dp", scatter_dimension=0, tiled=True).astype(f32)
    item_grad = jnp.dot(both_grad, gate_up.T, preferred_element_type=f32).astype(bf16)
    token_grad = lax.psum_scatter(item_grad, "expert", scatter_dimension=0, tiled=True)
    m_flat = first_moment[0].reshape(own_rows, width)
    v_flat = second_moment[0].reshape(own_rows, width)
    new_state = adam(w_flat.astype(f32), m_flat.astype(f32), v_flat.astype(f32), grad_sum)
    share = own_rows // experts_here
    outs = []
    for part in new_state:
        pieces = part.astype(bf16).reshape(experts_here, share, width)
        spread = lax.all_to_all(pieces, "expert", split_axis=0, concat_axis=0, tiled=True)
        homed = lax.all_to_all(spread[partner], "expert", split_axis=0, concat_axis=0, tiled=True)
        outs.append(homed.reshape(weights.shape))
    return (mixed, token_grad, *outs)


def shards(*args):
    replica_rows = lax.axis_size("expert") * args[0].shape[0]
    if replica_rows <= 4096 and args[5].shape[1] % (16 * lax.axis_size("expert")) == 0:
        return shards_dense(*args)
    return shards_by_slot(*args)


def solution(mesh):
    in_specs = (
        P(("dp", "expert"), None),
        P(("dp", "expert"), None),
        P(("dp", "expert"), None),
        P(("dp", "expert"), None),
        P(),
        P("expert", "dp", None, None),
        P("expert", "dp", None, None),
        P("expert", "dp", None, None),
    )
    out_specs = (
        P(("dp", "expert"), None),
        P(("dp", "expert"), None),
        P("expert", "dp", None, None),
        P("expert", "dp", None, None),
        P("expert", "dp", None, None),
    )
    return jax.shard_map(shards, mesh=mesh, in_specs=in_specs, out_specs=out_specs, check_vma=False)
```

profile of v0, /device:TPU:15, one launch (start us, length us, event | category | flops | bytes accessed | tf_op | source)
XLA Modules:
  0.0 465.4 jit_solution(3843170583067933573)
XLA Ops:
  7.2 2.4 copy.29
  11.2 16.0 %all-gather = f32[256,128]{1,0:T(8,128)S(1)} all-gather(f32[16,128]{1,0:T(8,128)S(1)} %bitcast.29), channel_id=2, replica_groups=mesh['dp'=2,'expert'=16] {'expert'}, dimensions={0}, use_global_device_ids=true | all-gather | bytes 139264 | tf_op jit(solution)/shard_map/all_gather | solution.py:167
  27.2 19.2 %all-gather.7.cloned.1.call-done = bf16[1024,1152]{0,1:T(8,128)(2,1)} async-done(((bf16[512,1152]{0,1:T(8,128)(2,1)}), bf16[1024,1152]{0,1:T(8,128)(2,1)}) %all-gather.7.cloned.1.call-update) | async-done | bytes 2359312 | tf_op jit(solution)/shard_map/all_gather | solution.py:164
  46.4 53.2 %all-gather.5.cloned.1.call-done = bf16[2048,1024]{1,0:T(8,128)(2,1)} async-done(((bf16[128,1024]{1,0:T(8,128)(2,1)}), bf16[2048,1024]{1,0:T(8,128)(2,1)}) %all-gather.5.cloned.1.call-update) | async-done | bytes 4194320 | tf_op jit(solution)/shard_map/all_gather | solution.py:165
  99.6 8.7 %fusion.14 = f32[2048,768]{0,1:T(8,128)} fusion(bf16[2048,1024]{1,0:T(8,128)(2,1)} %all-gather.5.cloned.1.call-done, bf16[1024,1152]{0,1:T(8,128)(2,1)} %all-gather.7.cloned.1.call-done), kind=kOutput, calls=%fused_computation.32 | convolution fusion | flops 3221225472 | bytes 12058624 | tf_op jit(solution)/shard_map/dot_general | solution.py:172
  108.4 42.5 %all-gather.9.cloned.1.call-done = bf16[2048,1024]{1,0:T(8,128)(2,1)} async-done(((bf16[128,1024]{1,0:T(8,128)(2,1)}), bf16[2048,1024]{1,0:T(8,128)(2,1)}) %all-gather.9.cloned.1.call-update) | async-done | bytes 4194320 | tf_op jit(solution)/shard_map/all_gather | solution.py:166
  150.9 7.5 %multiply_convert_fusion.3 = (bf16[2048,384]{0,1:T(8,128)(2,1)S(1)}, bf16[2048,384]{0,1:T(8,128)(2,1)S(1)}, bf16[2048,384]{0,1:T(8,128)(2,1)S(1)}) fusion(f32[2048,768]{0,1:T(8,128)} %fusion.14, bf16[1024,1152]{0,1:T(8,128)(2,1)} %all-gather.7.cloned.1.call-done, bf16[2048,1024]{1,0:T(8,128)(2,1)} %all-gather.9.cloned.1.call-done, f32[2048]{0:T(1024)S(1)} %bitcast.30), kind=kOutput, calls=%fused_computation.9 | convolution fusion | flops 1628700672 | bytes 15998976 | tf_op jit(solution)/shard_map/dot_general | solution.py:183
  162.2 3.4 fusion.10
  174.6 25.7 %reduce-scatter.8.cloned.1.call-done = bf16[512,1152]{0,1:T(8,128)(2,1)} async-done(((bf16[1024,1152]{0,1:T(8,128)(2,1)}), bf16[512,1152]{0,1:T(8,128)(2,1)}) %reduce-scatter.8.cloned.1.call-update) | async-done | bytes 1179664 | tf_op jit(solution)/shard_map/reduce_scatter | solution.py:190
  200.3 5.8 %fusion.16 = (bf16[512,1152]{0,1:T(8,128)(2,1)S(1)}, bf16[512,1152]{0,1:T(8,128)(2,1)}, bf16[512,1152]{0,1:T(8,128)(2,1)S(1)}) fusion(bf16[512,1152]{0,1:T(8,128)(2,1)} %reduce-scatter.8.cloned.1.call-done, f32[1,512,3,384]{1,3,2,0:T(8,128)} %copy.31, f32[1,512,3,384]{1,3,2,0:T(8,128)} %copy.30, bf16[1,512,3,384]{1,3,2,0:T(8,128)(2,1)S(1)} %copy-done), kind=kLoop, calls=%fused_computation.34 | loop fusion | flops 10616832 | bytes 10616832 | tf_op jit(solution)/shard_map/convert_element_type | solution.py:199
  208.5 6.4 %all-to-all-start = ((bf16[16,32,1152]{2,1,0:T(8,128)(2,1)}), bf16[16,32,1152]{2,1,0:T(8,128)(2,1)S(1)}, u32[]{:S(2)}, u32[]{:S(2)}) async-start(bf16[16,32,1152]{2,1,0:T(8,128)(2,1)} %bitcast.7), calls=%async_computation.3 | async-start | bytes 2359296 | tf_op jit(solution)/shard_map/all_to_all | solution.py:200
  214.9 7.8 %convolution_convert_fusion = bf16[2048,1024]{1,0:T(8,128)(2,1)} fusion(bf16[2048,384]{0,1:T(8,128)(2,1)} %copy-done.11, bf16[2048,384]{0,1:T(8,128)(2,1)} %copy-done.10, bf16[1024,1152]{0,1:T(8,128)(2,1)} %all-gather.7.cloned.1.call-done), kind=kOutput, calls=%fused_computation.5 | convolution fusion | flops 3229614080 | bytes 8912896 | tf_op jit(solution)/shard_map/dot_general | solution.py:191
  224.1 18.5 %all-to-all-done = bf16[16,32,1152]{2,1,0:T(8,128)(2,1)S(1)} async-done(((bf16[16,32,1152]{2,1,0:T(8,128)(2,1)}), bf16[16,32,1152]{2,1,0:T(8,128)(2,1)S(1)}, u32[]{:S(2)}, u32[]{:S(2)}) %all-to-all-start) | async-done | bytes 1179680 | tf_op jit(solution)/shard_map/all_to_all | solution.py:200
  242.6 4.9 %all-to-all-start.2 = ((bf16[16,32,1152]{2,1,0:T(8,128)(2,1)}), bf16[16,32,1152]{2,1,0:T(8,128)(2,1)S(1)}, u32[]{:S(2)}, u32[]{:S(2)}) async-start(bf16[16,32,1152]{2,1,0:T(8,128)(2,1)} %bitcast.8), calls=%async_computation.5 | async-start | bytes 2359296 | tf_op jit(solution)/shard_map/all_to_all | solution.py:200
  248.9 43.1 %all-to-all-done.2 = bf16[16,32,1152]{2,1,0:T(8,128)(2,1)S(1)} async-done(((bf16[16,32,1152]{2,1,0:T(8,128)(2,1)}), bf16[16,32,1152]{2,1,0:T(8,128)(2,1)S(1)}, u32[]{:S(2)}, u32[]{:S(2)}) %all-to-all-start.2) | async-done | bytes 1179680 | tf_op jit(solution)/shard_map/all_to_all | solution.py:200
  292.1 4.9 %all-to-all-start.4 = ((bf16[16,32,1152]{2,1,0:T(8,128)(2,1)}), bf16[16,32,1152]{2,1,0:T(8,128)(2,1)S(1)}, u32[]{:S(2)}, u32[]{:S(2)}) async-start(bf16[16,32,1152]{2,1,0:T(8,128)(2,1)} %bitcast.27), calls=%async_computation.7 | async-start | bytes 2359296 | tf_op jit(solution)/shard_map/all_to_all | solution.py:200
  298.6 33.8 %all-to-all-done.4 = bf16[16,32,1152]{2,1,0:T(8,128)(2,1)S(1)} async-done(((bf16[16,32,1152]{2,1,0:T(8,128)(2,1)}), bf16[16,32,1152]{2,1,0:T(8,128)(2,1)S(1)}, u32[]{:S(2)}, u32[]{:S(2)}) %all-to-all-start.4) | async-done | bytes 1179680 | tf_op jit(solution)/shard_map/all_to_all | solution.py:200
  332.4 5.1 %all-to-all-start.1 = ((bf16[16,32,1152]{2,1,0:T(8,128)(2,1)}), bf16[16,32,1152]{2,1,0:T(8,128)(2,1)S(1)}, u32[]{:S(2)}, u32[]{:S(2)}) async-start(bf16[16,32,1152]{2,1,0:T(8,128)(2,1)} %gather_fusion), calls=%async_computation.4 | async-start | bytes 2359296 | tf_op jit(solution)/shard_map/all_to_all | solution.py:201
  337.5 6.0 %multiply_convert_fusion.1 = bf16[2048,1024]{1,0:T(8,128)(2,1)} fusion(bf16[2048,384]{0,1:T(8,128)(2,1)} %copy-done.9, f32[2048]{0:T(1024)S(1)} %bitcast.32, bf16[1024,1152]{0,1:T(8,128)(2,1)} %all-gather.7.cloned.1.call-done), kind=kOutput, calls=%fused_computation.4 | convolution fusion | flops 1614807040 | bytes 6561792 | tf_op jit(solution)/shard_map/dot_general | solution.py:178
  345.2 20.0 %all-to-all-done.1 = bf16[16,32,1152]{2,1,0:T(8,128)(2,1)S(1)} async-done(((bf16[16,32,1152]{2,1,0:T(8,128)(2,1)}), bf16[16,32,1152]{2,1,0:T(8,128)(2,1)S(1)}, u32[]{:S(2)}, u32[]{:S(2)}) %all-to-all-start.1) | async-done | bytes 1179680 | tf_op jit(solution)/shard_map/all_to_all | solution.py:201
  365.2 4.9 %all-to-all-start.3 = ((bf16[16,32,1152]{2,1,0:T(8,128)(2,1)}), bf16[16,32,1152]{2,1,0:T(8,128)(2,1)}, u32[]{:S(2)}, u32[]{:S(2)}) async-start(bf16[16,32,1152]{2,1,0:T(8,128)(2,1)} %gather_fusion.1), calls=%async_computation.6 | async-start | bytes 2359296 | tf_op jit(solution)/shard_map/all_to_all | solution.py:201
  371.8 43.0 %all-to-all-done.3 = bf16[16,32,1152]{2,1,0:T(8,128)(2,1)} async-done(((bf16[16,32,1152]{2,1,0:T(8,128)(2,1)}), bf16[16,32,1152]{2,1,0:T(8,128)(2,1)}, u32[]{:S(2)}, u32[]{:S(2)}) %all-to-all-start.3) | async-done | bytes 1179680 | tf_op jit(solution)/shard_map/all_to_all | solution.py:201
  414.8 5.0 %all-to-all-start.5 = ((bf16[16,32,1152]{2,1,0:T(8,128)(2,1)}), bf16[16,32,1152]{2,1,0:T(8,128)(2,1)}, u32[]{:S(2)}, u32[]{:S(2)}) async-start(bf16[16,32,1152]{2,1,0:T(8,128)(2,1)} %gather_fusion.2), calls=%async_computation.8 | async-start | bytes 2359296 | tf_op jit(solution)/shard_map/all_to_all | solution.py:201
  424.7 30.4 %all-to-all-done.5 = bf16[16,32,1152]{2,1,0:T(8,128)(2,1)} async-done(((bf16[16,32,1152]{2,1,0:T(8,128)(2,1)}), bf16[16,32,1152]{2,1,0:T(8,128)(2,1)}, u32[]{:S(2)}, u32[]{:S(2)}) %all-to-all-start.5) | async-done | bytes 1179680 | tf_op jit(solution)/shard_map/all_to_all | solution.py:201
  (60 shorter events, 33.0 us)
Async XLA Ops:
  7.2 4.0 copy-start.5
  7.2 4.0 copy-start.4
  7.2 39.2 %all-gather.7.cloned.1.call-start = ((), (), s32[]{:S(2)}) async-start(), calls=%async_computation.10 | async-start | bytes 3538944 | tf_op jit(solution)/shard_map/all_gather | solution.py:164
  9.6 90.0 %all-gather.5.cloned.1.call-start = ((), (), s32[]{:S(2)}) async-start(), calls=%async_computation.9 | async-start | bytes 4456448 | tf_op jit(solution)/shard_map/all_gather | solution.py:165
  10.4 140.5 %all-gather.9.cloned.1.call-start = ((), (), s32[]{:S(2)}) async-start(), calls=%async_computation.12 | async-start | bytes 4456448 | tf_op jit(solution)/shard_map/all_gather | solution.py:166
  11.1 189.2 %reduce-scatter.8.cloned.1.call-start = ((), (), s32[]{:S(2)}) async-start(), calls=%async_computation.14 | async-start | bytes 3538944 | tf_op jit(solution)/shard_map/reduce_scatter | solution.py:190
  150.9 7.5 %copy-start.7 = (bf16[2048,1024]{1,0:T(8,128)(2,1)S(1)}, bf16[2048,1024]{1,0:T(8,128)(2,1)}, u32[]{:S(2)}) copy-start(bf16[2048,1024]{1,0:T(8,128)(2,1)} %all-gather.9.cloned.1.call-done) | copy-start | bytes 12582916
  158.3 2.0 copy-start.9
  158.3 2.0 copy-start.10
  158.4 2.4 copy-start.11
  158.4 3.9 copy-start.6
  167.3 1.3 copy-start.3
  172.6 27.7 %copy-start = (bf16[1,512,3,384]{1,3,2,0:T(8,128)(2,1)S(1)}, bf16[1,512,3,384]{1,3,2,0:T(8,128)(2,1)}, u32[]{:S(2)}) copy-start(bf16[1,512,3,384]{1,3,2,0:T(8,128)(2,1)} %copy.29) | copy-start | bytes 3538948
  208.5 34.1 %all-to-all-start = ((bf16[16,32,1152]{2,1,0:T(8,128)(2,1)}), bf16[16,32,1152]{2,1,0:T(8,128)(2,1)S(1)}, u32[]{:S(2)}, u32[]{:S(2)}) async-start(bf16[16,32,1152]{2,1,0:T(8,128)(2,1)} %bitcast.7), calls=%async_computation.3 | async-start | bytes 2359296 | tf_op jit(solution)/shard_map/all_to_all | solution.py:200
  214.9 243.7 %reduce-scatter.6.cloned.1.call-start = ((), (), s32[]{:S(2)}) async-start(), calls=%async_computation.13 | async-start | bytes 4456448 | tf_op jit(solution)/shard_map/reduce_scatter | solution.py:192
  242.6 49.4 %all-to-all-start.2 = ((bf16[16,32,1152]{2,1,0:T(8,128)(2,1)}), bf16[16,32,1152]{2,1,0:T(8,128)(2,1)S(1)}, u32[]{:S(2)}, u32[]{:S(2)}) async-start(bf16[16,32,1152]{2,1,0:T(8,128)(2,1)} %bitcast.8), calls=%async_computation.5 | async-start | bytes 2359296 | tf_op jit(solution)/shard_map/all_to_all | solution.py:200
  247.5 49.4 %copy-start.8 = (s32[16]{0:T(128)S(1)}, s32[16]{0:T(128)}, u32[]{:S(2)}) copy-start(s32[16]{0:T(128)} %param.12) | copy-start | bytes 196
  292.1 40.4 %all-to-all-start.4 = ((bf16[16,32,1152]{2,1,0:T(8,128)(2,1)}), bf16[16,32,1152]{2,1,0:T(8,128)(2,1)S(1)}, u32[]{:S(2)}, u32[]{:S(2)}) async-start(bf16[16,32,1152]{2,1,0:T(8,128)(2,1)} %bitcast.27), calls=%async_computation.7 | async-start | bytes 2359296 | tf_op jit(solution)/shard_map/all_to_all | solution.py:200
  332.4 32.8 %all-to-all-start.1 = ((bf16[16,32,1152]{2,1,0:T(8,128)(2,1)}), bf16[16,32,1152]{2,1,0:T(8,128)(2,1)S(1)}, u32[]{:S(2)}, u32[]{:S(2)}) async-start(bf16[16,32,1152]{2,1,0:T(8,128)(2,1)} %gather_fusion), calls=%async_computation.4 | async-start | bytes 2359296 | tf_op jit(solution)/shard_map/all_to_all | solution.py:201
  337.5 121.1 %reduce-scatter.4.cloned.1.call-start = ((), (), s32[]{:S(2)}) async-start(), calls=%async_computation.11 | async-start | bytes 4456448 | tf_op jit(solution)/shard_map/reduce_scatter | solution.py:179
  365.2 6.6 %copy-start.1 = (bf16[16,32,1152]{2,1,0:T(8,128)(2,1)}, bf16[16,32,1152]{2,1,0:T(8,128)(2,1)S(1)}, u32[]{:S(2)}) copy-start(bf16[16,32,1152]{2,1,0:T(8,128)(2,1)S(1)} %all-to-all-done.1) | copy-start | bytes 3538948
  365.2 49.5 %all-to-all-start.3 = ((bf16[16,32,1152]{2,1,0:T(8,128)(2,1)}), bf16[16,32,1152]{2,1,0:T(8,128)(2,1)}, u32[]{:S(2)}, u32[]{:S(2)}) async-start(bf16[16,32,1152]{2,1,0:T(8,128)(2,1)} %gather_fusion.1), calls=%async_computation.6 | async-start | bytes 2359296 | tf_op jit(solution)/shard_map/all_to_all | solution.py:201
  414.8 5.0 %copy-start.2 = (bf16[16,32,1152]{2,1,0:T(8,128)(2,1)S(1)}, bf16[16,32,1152]{2,1,0:T(8,128)(2,1)}, u32[]{:S(2)}) copy-start(bf16[16,32,1152]{2,1,0:T(8,128)(2,1)} %copy-done.1) | copy-start | bytes 3538948
  414.8 40.4 %all-to-all-start.5 = ((bf16[16,32,1152]{2,1,0:T(8,128)(2,1)}), bf16[16,32,1152]{2,1,0:T(8,128)(2,1)}, u32[]{:S(2)}, u32[]{:S(2)}) async-start(bf16[16,32,1152]{2,1,0:T(8,128)(2,1)} %gather_fusion.2), calls=%async_computation.8 | async-start | bytes 2359296 | tf_op jit(solution)/shard_map/all_to_all | solution.py:201
Sparse Core Ops, SparseCore 0:
  10.1 36.2 all-gather.6
  48.6 50.9 all-gather.4
  101.8 49.0 all-gather.8
  167.5 32.7 reduce-scatter.7
  222.9 95.5 reduce-scatter.5
  343.7 96.6 reduce-scatter.3
where the time goes:
time: 466 us; the launch traced here: 465 us
  waiting for transfers between devices  331 us (71%)
  matrix products  35.4 us (8%)
  starting transfers between devices  31.2 us (7%)
  local copies, waits for them, and re-layouts  28.5 us (6%)
  blocking collectives  16 us (3%)
  between operations  14.3 us (3%)
  other arithmetic  9.17 us (2%)
    all_to_all x3, waiting for transfers between devices, shards_dense(): lax.all_to_all(pieces, 'expert', split_axis=0, concat_axis=0, tiled=True)  95.4 us
    all_to_all x3, waiting for transfers between devices, shards_dense(): lax.all_to_all(spread[partner], 'expert', split_axis=0, concat_axis=0, ti...  93.4 us
    all_gather x1, waiting for transfers between devices, shards_dense(): x_rows = lax.all_gather(tokens, 'expert', axis=0, tiled=True)  53.2 us
    all_gather x1, waiting for transfers between devices, shards_dense(): cot_rows = lax.all_gather(cotangent, 'expert', axis=0, tiled=True)  42.5 us
    reduce_scatter x1, waiting for transfers between devices, shards_dense(): lax.psum_scatter(partial, 'dp', scatter_dimension=0, tiled=True).astype(f32)  25.7 us
    all_gather x1, waiting for transfers between devices, shards_dense(): gathered = lax.all_gather(w_flat, 'dp', axis=0, tiled=True)  19.2 us
    all_to_all x3, starting transfers between devices, shards_dense(): lax.all_to_all(pieces, 'expert', split_axis=0, concat_axis=0, tiled=True)  16.1 us
    all_gather x1, blocking collectives, shards_dense(): gate_all = lax.all_gather(gate_table, 'expert', axis=0)  16 us
  transfers between devices with their start and end apart: 12, of which 10 were waited for; matrix products, arithmetic and copies ran while one was open for 10% of the time, Pallas kernels for 0%

commit v1 on v0

--- a/solution.py
+++ b/solution.py
@@ -1,3 +1,4 @@
+import functools
 import jax
 import jax.numpy as jnp
 from jax import lax
@@ -9,6 +10,39 @@
 decay_rate = 0.1
 eps_adam = 1e-08
 step_count = 100
+
+
+def clear_the_sums_all(u_in, join_dim, frame_in):
+    n_now, b_now = (u_in.shape[:join_dim], u_in.shape[join_dim + 1 :])
+    response = u_in.reshape(*n_now, frame_in, -1, *b_now)
+    return jnp.moveaxis(response, join_dim, 0)
+
+
+def choose_the_rings(array_here, along_dim):
+    array_here = jnp.moveaxis(array_here, 0, along_dim)
+    left_arr = array_here.shape
+    return array_here.reshape(
+        *left_arr[:along_dim],
+        left_arr[along_dim] * left_arr[along_dim + 1],
+        *left_arr[along_dim + 2 :]
+    )
+
+
+def launch_pieces_all_up(arr, link_axis, x_in, q_in):
+    u_next = lax.axis_size(link_axis)
+    last = lax.axis_index(link_axis)
+    later, small = (u_next, last)
+    ready = clear_the_sums_all(arr, x_in, later)
+    earlier = ready
+    for k in tuple(range(1, later)):
+        val, mat_out = ((small + k) % later, (small - k) % later)
+        reached = lax.dynamic_index_in_dim(ready, val, 0)
+        s_next = lax.ppermute(reached, link_axis, [(c, (c + k) % later) for c in range(later)])
+        earlier = lax.dynamic_update_slice_in_dim(earlier, s_next, mat_out, axis=0)
+    return choose_the_rings(earlier, q_in)
+
+
+assign_sections = functools.partial(launch_pieces_all_up, link_axis="expert", x_in=0, q_in=0)
 
 
 def send_rows(parts):
@@ -197,7 +231,7 @@
     outs = []
     for part in new_state:
         pieces = part.astype(bf16).reshape(experts_here, share, width)
-        spread = lax.all_to_all(pieces, "expert", split_axis=0, concat_axis=0, tiled=True)
+        spread = assign_sections(pieces)
         homed = lax.all_to_all(spread[partner], "expert", split_axis=0, concat_axis=0, tiled=True)
         outs.append(homed.reshape(weights.shape))
     return (mixed, token_grad, *outs)

time: 466 us -> 451 us (0.968)
  waiting for transfers between devices: 331 us -> 239 us
  starting transfers between devices: 31.2 us -> 90 us
  local copies, waits for them, and re-layouts: 28.5 us -> 43.6 us
    all_to_all x3 -> x0, waiting for transfers between devices: 95.4 us -> none  [shards_dense(): lax.all_to_all(pieces, 'expert', split_axis=0, concat_axis=0, tiled=True)]
    ppermute x0 -> x45, starting transfers between devices: none -> 68.2 us  [launch_pieces_all_up(): lax.ppermute(reached, link_axis, [(c, (c + k) % later) for c in range(lat...]
    ppermute x0 -> x45, waiting for transfers between devices: none -> 49.7 us  [launch_pieces_all_up(): lax.ppermute(reached, link_axis, [(c, (c + k) % later) for c in range(lat...]
    all_to_all x3, waiting for transfers between devices: 93.4 us -> 60.3 us  [shards_dense(): lax.all_to_all(spread[partner], 'expert', split_axis=0, concat_axis=0, ti...]
    all_to_all x3 -> x0, starting transfers between devices: 16.1 us -> none  [shards_dense(): lax.all_to_all(pieces, 'expert', split_axis=0, concat_axis=0, tiled=True)]
    dynamic_update_slice x0 -> x45, local copies, waits for them, and re-layouts: none -> 14 us  [launch_pieces_all_up(): earlier = lax.dynamic_update_slice_in_dim(earlier, s_next, mat_out, axis=0)]
    reduce_scatter x1, waiting for transfers between devices: 25.7 us -> 13 us  [shards_dense(): lax.psum_scatter(partial, 'dp', scatter_dimension=0, tiled=True).astype(f32)]
    all_to_all x3, starting transfers between devices: 14.9 us -> 21.3 us  [shards_dense(): lax.all_to_all(spread[partner], 'expert', split_axis=0, concat_axis=0, ti...]
  transfers between devices with their start and end apart: 12 -> 54, of which waited for: 10 -> 16; matrix products, arithmetic and copies ran while one was open for 10% -> 15% of each run, Pallas kernels for 0% -> 0%
where the time goes in v1:
time: 451 us; the launch traced here: 448 us
  waiting for transfers between devices  239 us (53%)
  starting transfers between devices  90 us (20%)
  local copies, waits for them, and re-layouts  43.6 us (10%)
  matrix products  35.1 us (8%)
  blocking collectives  16 us (4%)
  between operations  15.4 us (3%)
  other arithmetic  8.59 us (2%)
    ppermute x45, starting transfers between devices, launch_pieces_all_up(): lax.ppermute(reached, link_axis, [(c, (c + k) % later) for c in range(lat...  68.2 us
    all_to_all x3, waiting for transfers between devices, shards_dense(): lax.all_to_all(spread[partner], 'expert', split_axis=0, concat_axis=0, ti...  60.3 us
    all_gather x1, waiting for transfers between devices, shards_dense(): x_rows = lax.all_gather(tokens, 'expert', axis=0, tiled=True)  53.2 us
    ppermute x45, waiting for transfers between devices, launch_pieces_all_up(): lax.ppermute(reached, link_axis, [(c, (c + k) % later) for c in range(lat...  49.7 us
    all_gather x1, waiting for transfers between devices, shards_dense(): cot_rows = lax.all_gather(cotangent, 'expert', axis=0, tiled=True)  42.5 us
    all_to_all x3, starting transfers between devices, shards_dense(): lax.all_to_all(spread[partner], 'expert', split_axis=0, concat_axis=0, ti...  21.3 us
    all_gather x1, waiting for transfers between devices, shards_dense(): gathered = lax.all_gather(w_flat, 'dp', axis=0, tiled=True)  19.2 us
    all_gather x1, blocking collectives, shards_dense(): gate_all = lax.all_gather(gate_table, 'expert', axis=0)  16 us
  transfers between devices with their start and end apart: 54, of which 16 were waited for; matrix products, arithmetic and copies ran while one was open for 15% of the time, Pallas kernels for 0%

profile of v1, /device:TPU:15, one launch (start us, length us, event | category | flops | bytes accessed | tf_op | source)
XLA Modules:
  0.0 447.9 jit_solution(9371415144126121954)
XLA Ops:
  11.2 16.0 %all-gather = f32[256,128]{1,0:T(8,128)S(1)} all-gather(f32[16,128]{1,0:T(8,128)S(1)} %bitcast.127), channel_id=2, replica_groups=mesh['dp'=2,'expert'=16] {'expert'}, dimensions={0}, use_global_device_ids=true | all-gather | bytes 139264 | tf_op jit(solution)/shard_map/all_gather | solution.py:201
  27.2 19.2 %all-gather.7.cloned.1.call-done = bf16[1024,1152]{0,1:T(8,128)(2,1)} async-done(((bf16[512,1152]{0,1:T(8,128)(2,1)}), bf16[1024,1152]{0,1:T(8,128)(2,1)}) %all-gather.7.cloned.1.call-update) | async-done | bytes 2359312 | tf_op jit(solution)/shard_map/all_gather | solution.py:198
  46.4 53.2 %all-gather.5.cloned.1.call-done = bf16[2048,1024]{1,0:T(8,128)(2,1)} async-done(((bf16[128,1024]{1,0:T(8,128)(2,1)}), bf16[2048,1024]{1,0:T(8,128)(2,1)}) %all-gather.5.cloned.1.call-update) | async-done | bytes 4194320 | tf_op jit(solution)/shard_map/all_gather | solution.py:199
  99.6 8.7 %fusion.14 = f32[2048,768]{0,1:T(8,128)} fusion(bf16[2048,1024]{1,0:T(8,128)(2,1)} %all-gather.5.cloned.1.call-done, bf16[1024,1152]{0,1:T(8,128)(2,1)} %all-gather.7.cloned.1.call-done), kind=kOutput, calls=%fused_computation.32 | convolution fusion | flops 3221225472 | bytes 12058624 | tf_op jit(solution)/shard_map/dot_general | solution.py:206
  108.3 42.5 %all-gather.9.cloned.1.call-done = bf16[2048,1024]{1,0:T(8,128)(2,1)} async-done(((bf16[128,1024]{1,0:T(8,128)(2,1)}), bf16[2048,1024]{1,0:T(8,128)(2,1)}) %all-gather.9.cloned.1.call-update) | async-done | bytes 4194320 | tf_op jit(solution)/shard_map/all_gather | solution.py:200
  150.8 7.2 %multiply_convert_fusion.3 = (bf16[2048,384]{0,1:T(8,128)(2,1)S(1)}, bf16[2048,384]{0,1:T(8,128)(2,1)S(1)}, bf16[2048,384]{0,1:T(8,128)(2,1)S(1)}) fusion(f32[2048,768]{0,1:T(8,128)} %fusion.14, bf16[1024,1152]{0,1:T(8,128)(2,1)S(1)} %copy-done.33, bf16[2048,1024]{1,0:T(8,128)(2,1)} %all-gather.9.cloned.1.call-done, f32[2048]{0:T(1024)S(1)} %bitcast.128), kind=kOutput, calls=%fused_computation.9 | convolution fusion | flops 1628700672 | bytes 15998976 | tf_op jit(solution)/shard_map/dot_general | solution.py:217
  162.0 3.4 fusion.10
  167.3 5.8 %multiply_convert_fusion.1 = bf16[2048,1024]{1,0:T(8,128)(2,1)} fusion(bf16[2048,384]{0,1:T(8,128)(2,1)} %copy-done.35, f32[2048]{0:T(1024)S(1)} %bitcast.130, bf16[1024,1152]{0,1:T(8,128)(2,1)S(1)} %copy-done.33), kind=kOutput, calls=%fused_computation.4 | convolution fusion | flops 1614807040 | bytes 6561792 | tf_op jit(solution)/shard_map/dot_general | solution.py:212
  179.0 7.9 %convolution_convert_fusion = bf16[2048,1024]{1,0:T(8,128)(2,1)} fusion(bf16[2048,384]{0,1:T(8,128)(2,1)} %copy-done.37, bf16[2048,384]{0,1:T(8,128)(2,1)} %copy-done.36, bf16[1024,1152]{0,1:T(8,128)(2,1)} %all-gather.7.cloned.1.call-done), kind=kOutput, calls=%fused_computation.5 | convolution fusion | flops 3229614080 | bytes 8912896 | tf_op jit(solution)/shard_map/dot_general | solution.py:225
  187.0 13.0 %reduce-scatter.8.cloned.1.call-done = bf16[512,1152]{0,1:T(8,128)(2,1)} async-done(((bf16[1024,1152]{0,1:T(8,128)(2,1)}), bf16[512,1152]{0,1:T(8,128)(2,1)}) %reduce-scatter.8.cloned.1.call-update) | async-done | bytes 1179664 | tf_op jit(solution)/shard_map/reduce_scatter | solution.py:224
  200.0 6.6 %fusion.16 = (bf16[512,1152]{0,1:T(8,128)(2,1)}, bf16[512,1152]{0,1:T(8,128)(2,1)}, bf16[512,1152]{0,1:T(8,128)(2,1)}) fusion(bf16[512,1152]{0,1:T(8,128)(2,1)} %reduce-scatter.8.cloned.1.call-done, f32[1,512,3,384]{1,3,2,0:T(8,128)S(1)} %copy-done.1, f32[1,512,3,384]{1,3,2,0:T(8,128)} %copy.78, bf16[1,512,3,384]{1,3,2,0:T(8,128)(2,1)S(1)} %copy-done), kind=kLoop, calls=%fused_computation.34 | loop fusion | flops 10616832 | bytes 10616832 | tf_op jit(solution)/shard_map/convert_element_type | solution.py:233
  213.4 2.9 collective-permute-start.4
  240.7 5.0 %collective-permute-start.15 = (bf16[1,1,32,1152]{3,2,0,1:T(8,128)(2,1)}, bf16[1,1,32,1152]{3,2,0,1:T(8,128)(2,1)}, u32[]{:S(2)}, u32[]{:S(2)}) collective-permute-start(bf16[1,1,32,1152]{3,2,0,1:T(8,128)(2,1)} %get-tuple-element.50), channel_id=1, source_target_pairs={{0,1},{1,2},{2,3},{3,4},{4,5},{5,6},{6,7},{7,8},{8,9},{9,10},{10,1... | collective-permute-start | bytes 221192 | tf_op jit(solution)/shard_map/ppermute | solution.py:40
  249.0 5.0 %collective-permute-done.13 = bf16[1,1,32,1152]{3,2,0,1:T(8,128)(2,1)S(1)} collective-permute-done((bf16[1,1,32,1152]{3,2,0,1:T(8,128)(2,1)S(1)}, bf16[1,1,32,1152]{3,2,0,1:T(8,128)(2,1)S(1)}, u32[]{:S(2)}, u32[]{:S(2)}) %collective-permute-start.13) | collective-permute-done | bytes 73760 | tf_op jit(solution)/shard_map/ppermute | solution.py:40
  258.5 5.7 %all-to-all-start = ((bf16[16,32,1152]{2,1,0:T(8,128)(2,1)}), bf16[16,32,1152]{2,1,0:T(8,128)(2,1)S(1)}, u32[]{:S(2)}, u32[]{:S(2)}) async-start(bf16[16,32,1152]{2,1,0:T(8,128)(2,1)} %gather_fusion), calls=%async_computation.3 | async-start | bytes 2359296 | tf_op jit(solution)/shard_map/all_to_all | solution.py:235
  273.5 3.0 collective-permute-start.24
  277.5 32.2 %collective-permute-done.20 = bf16[1,1,32,1152]{3,2,0,1:T(8,128)(2,1)S(1)} collective-permute-done((bf16[1,1,32,1152]{3,2,0,1:T(8,128)(2,1)}, bf16[1,1,32,1152]{3,2,0,1:T(8,128)(2,1)S(1)}, u32[]{:S(2)}, u32[]{:S(2)}) %collective-permute-start.20) | collective-permute-done | bytes 73760 | tf_op jit(solution)/shard_map/ppermute | solution.py:40
  334.0 5.7 %collective-permute-done.35 = bf16[1,1,32,1152]{3,2,0,1:T(8,128)(2,1)S(1)} collective-permute-done((bf16[1,1,32,1152]{3,2,0,1:T(8,128)(2,1)S(1)}, bf16[1,1,32,1152]{3,2,0,1:T(8,128)(2,1)S(1)}, u32[]{:S(2)}, u32[]{:S(2)}) %collective-permute-start.35) | collective-permute-done | bytes 73760 | tf_op jit(solution)/shard_map/ppermute | solution.py:40
  339.7 4.2 collective-permute-start.40
  344.4 3.1 collective-permute-start.43
  350.8 10.3 %all-to-all-start.1 = ((bf16[16,32,1152]{2,1,0:T(8,128)(2,1)}), bf16[16,32,1152]{2,1,0:T(8,128)(2,1)S(1)}, u32[]{:S(2)}, u32[]{:S(2)}) async-start(bf16[16,32,1152]{2,1,0:T(8,128)(2,1)} %gather_fusion.1), calls=%async_computation.4 | async-start | bytes 2359296 | tf_op jit(solution)/shard_map/all_to_all | solution.py:235
  367.4 36.1 %all-to-all-done.1 = bf16[16,32,1152]{2,1,0:T(8,128)(2,1)S(1)} async-done(((bf16[16,32,1152]{2,1,0:T(8,128)(2,1)}), bf16[16,32,1152]{2,1,0:T(8,128)(2,1)S(1)}, u32[]{:S(2)}, u32[]{:S(2)}) %all-to-all-start.1) | async-done | bytes 1179680 | tf_op jit(solution)/shard_map/all_to_all | solution.py:235
  404.5 5.3 %all-to-all-start.2 = ((bf16[16,32,1152]{2,1,0:T(8,128)(2,1)}), bf16[16,32,1152]{2,1,0:T(8,128)(2,1)}, u32[]{:S(2)}, u32[]{:S(2)}) async-start(bf16[16,32,1152]{2,1,0:T(8,128)(2,1)} %gather_fusion.2), calls=%async_computation.5 | async-start | bytes 2359296 | tf_op jit(solution)/shard_map/all_to_all | solution.py:235
  413.5 24.2 %all-to-all-done.2 = bf16[16,32,1152]{2,1,0:T(8,128)(2,1)} async-done(((bf16[16,32,1152]{2,1,0:T(8,128)(2,1)}), bf16[16,32,1152]{2,1,0:T(8,128)(2,1)}, u32[]{:S(2)}, u32[]{:S(2)}) %all-to-all-start.2) | async-done | bytes 1179680 | tf_op jit(solution)/shard_map/all_to_all | solution.py:235
  (244 shorter events, 106.2 us)
Async XLA Ops:
  7.2 39.2 %all-gather.7.cloned.1.call-start = ((), (), s32[]{:S(2)}) async-start(), calls=%async_computation.7 | async-start | bytes 3538944 | tf_op jit(solution)/shard_map/all_gather | solution.py:198
  9.6 90.0 %all-gather.5.cloned.1.call-start = ((), (), s32[]{:S(2)}) async-start(), calls=%async_computation.6 | async-start | bytes 4456448 | tf_op jit(solution)/shard_map/all_gather | solution.py:199
  10.4 140.5 %all-gather.9.cloned.1.call-start = ((), (), s32[]{:S(2)}) async-start(), calls=%async_computation.9 | async-start | bytes 4456448 | tf_op jit(solution)/shard_map/all_gather | solution.py:200
  11.1 188.9 %reduce-scatter.8.cloned.1.call-start = ((), (), s32[]{:S(2)}) async-start(), calls=%async_computation.11 | async-start | bytes 3538944 | tf_op jit(solution)/shard_map/reduce_scatter | solution.py:224
  167.1 274.0 %reduce-scatter.4.cloned.1.call-start = ((), (), s32[]{:S(2)}) async-start(), calls=%async_computation.8 | async-start | bytes 4456448 | tf_op jit(solution)/shard_map/reduce_scatter | solution.py:213
  173.1 268.0 %reduce-scatter.6.cloned.1.call-start = ((), (), s32[]{:S(2)}) async-start(), calls=%async_computation.10 | async-start | bytes 4456448 | tf_op jit(solution)/shard_map/reduce_scatter | solution.py:226
  240.7 23.7 %collective-permute-start.15 = (bf16[1,1,32,1152]{3,2,0,1:T(8,128)(2,1)}, bf16[1,1,32,1152]{3,2,0,1:T(8,128)(2,1)}, u32[]{:S(2)}, u32[]{:S(2)}) collective-permute-start(bf16[1,1,32,1152]{3,2,0,1:T(8,128)(2,1)} %get-tuple-element.50), channel_id=1, source_target_pairs={{0,1},{1,2},{2,3},{3,4},{4,5},{5,6},{6,7},{7,8},{8,9},{9,10},{10,1... | collective-permute-start | bytes 221192 | tf_op jit(solution)/shard_map/ppermute | solution.py:40
  245.7 21.7 %collective-permute-start.16 = (bf16[1,1,32,1152]{3,2,0,1:T(8,128)(2,1)}, bf16[1,1,32,1152]{3,2,0,1:T(8,128)(2,1)}, u32[]{:S(2)}, u32[]{:S(2)}) collective-permute-start(bf16[1,1,32,1152]{3,2,0,1:T(8,128)(2,1)} %get-tuple-element.49), channel_id=1, source_target_pairs={{0,2},{1,3},{2,4},{3,5},{4,6},{5,7},{6,8},{7,9},{8,10},{9,11},{10,... | collective-permute-start | bytes 221192 | tf_op jit(solution)/shard_map/ppermute | solution.py:40
  249.0 20.2 %collective-permute-start.17 = (bf16[1,1,32,1152]{3,2,0,1:T(8,128)(2,1)}, bf16[1,1,32,1152]{3,2,0,1:T(8,128)(2,1)}, u32[]{:S(2)}, u32[]{:S(2)}) collective-permute-start(bf16[1,1,32,1152]{3,2,0,1:T(8,128)(2,1)} %get-tuple-element.48), channel_id=1, source_target_pairs={{0,3},{1,4},{2,5},{3,6},{4,7},{5,8},{6,9},{7,10},{8,11},{9,12},{10... | collective-permute-start | bytes 221192 | tf_op jit(solution)/shard_map/ppermute | solution.py:40
  254.0 18.2 %collective-permute-start.18 = (bf16[1,1,32,1152]{3,2,0,1:T(8,128)(2,1)}, bf16[1,1,32,1152]{3,2,0,1:T(8,128)(2,1)}, u32[]{:S(2)}, u32[]{:S(2)}) collective-permute-start(bf16[1,1,32,1152]{3,2,0,1:T(8,128)(2,1)} %get-tuple-element.47), channel_id=1, source_target_pairs={{0,4},{1,5},{2,6},{3,7},{4,8},{5,9},{6,10},{7,11},{8,12},{9,13},{1... | collective-permute-start | bytes 221192 | tf_op jit(solution)/shard_map/ppermute | solution.py:40
  256.0 17.6 %collective-permute-start.19 = (bf16[1,1,32,1152]{3,2,0,1:T(8,128)(2,1)}, bf16[1,1,32,1152]{3,2,0,1:T(8,128)(2,1)}, u32[]{:S(2)}, u32[]{:S(2)}) collective-permute-start(bf16[1,1,32,1152]{3,2,0,1:T(8,128)(2,1)} %get-tuple-element.46), channel_id=1, source_target_pairs={{0,5},{1,6},{2,7},{3,8},{4,9},{5,10},{6,11},{7,12},{8,13},{9,14},{... | collective-permute-start | bytes 221192 | tf_op jit(solution)/shard_map/ppermute | solution.py:40
  258.5 92.3 %all-to-all-start = ((bf16[16,32,1152]{2,1,0:T(8,128)(2,1)}), bf16[16,32,1152]{2,1,0:T(8,128)(2,1)S(1)}, u32[]{:S(2)}, u32[]{:S(2)}) async-start(bf16[16,32,1152]{2,1,0:T(8,128)(2,1)} %gather_fusion), calls=%async_computation.3 | async-start | bytes 2359296 | tf_op jit(solution)/shard_map/all_to_all | solution.py:235
  264.3 45.3 %collective-permute-start.20 = (bf16[1,1,32,1152]{3,2,0,1:T(8,128)(2,1)}, bf16[1,1,32,1152]{3,2,0,1:T(8,128)(2,1)S(1)}, u32[]{:S(2)}, u32[]{:S(2)}) collective-permute-start(bf16[1,1,32,1152]{3,2,0,1:T(8,128)(2,1)} %get-tuple-element.45), channel_id=1, source_target_pairs={{0,6},{1,7},{2,8},{3,9},{4,10},{5,11},{6,12},{7,13},{8,14},{9,15},... | collective-permute-start | bytes 221192 | tf_op jit(solution)/shard_map/ppermute | solution.py:40
  267.4 43.8 %collective-permute-start.21 = (bf16[1,1,32,1152]{3,2,0,1:T(8,128)(2,1)}, bf16[1,1,32,1152]{3,2,0,1:T(8,128)(2,1)S(1)}, u32[]{:S(2)}, u32[]{:S(2)}) collective-permute-start(bf16[1,1,32,1152]{3,2,0,1:T(8,128)(2,1)} %get-tuple-element.44), channel_id=1, source_target_pairs={{0,7},{1,8},{2,9},{3,10},{4,11},{5,12},{6,13},{7,14},{8,15},{9,0},... | collective-permute-start | bytes 221192 | tf_op jit(solution)/shard_map/ppermute | solution.py:40
  269.2 43.6 %collective-permute-start.22 = (bf16[1,1,32,1152]{3,2,0,1:T(8,128)(2,1)}, bf16[1,1,32,1152]{3,2,0,1:T(8,128)(2,1)S(1)}, u32[]{:S(2)}, u32[]{:S(2)}) collective-permute-start(bf16[1,1,32,1152]{3,2,0,1:T(8,128)(2,1)} %get-tuple-element.43), channel_id=1, source_target_pairs={{0,8},{1,9},{2,10},{3,11},{4,12},{5,13},{6,14},{7,15},{8,0},{9,1},... | collective-permute-start | bytes 221192 | tf_op jit(solution)/shard_map/ppermute | solution.py:40
  272.3 43.2 %collective-permute-start.23 = (bf16[1,1,32,1152]{3,2,0,1:T(8,128)(2,1)}, bf16[1,1,32,1152]{3,2,0,1:T(8,128)(2,1)S(1)}, u32[]{:S(2)}, u32[]{:S(2)}) collective-permute-start(bf16[1,1,32,1152]{3,2,0,1:T(8,128)(2,1)} %get-tuple-element.42), channel_id=1, source_target_pairs={{0,9},{1,10},{2,11},{3,12},{4,13},{5,14},{6,15},{7,0},{8,1},{9,2},... | collective-permute-start | bytes 221192 | tf_op jit(solution)/shard_map/ppermute | solution.py:40
  273.5 44.7 %collective-permute-start.24 = (bf16[1,1,32,1152]{3,2,0,1:T(8,128)(2,1)}, bf16[1,1,32,1152]{3,2,0,1:T(8,128)(2,1)S(1)}, u32[]{:S(2)}, u32[]{:S(2)}) collective-permute-start(bf16[1,1,32,1152]{3,2,0,1:T(8,128)(2,1)} %get-tuple-element.41), channel_id=1, source_target_pairs={{0,10},{1,11},{2,12},{3,13},{4,14},{5,15},{6,0},{7,1},{8,2},{9,3},... | collective-permute-start | bytes 221192 | tf_op jit(solution)/shard_map/ppermute | solution.py:40
  339.7 21.5 %collective-permute-start.40 = (bf16[1,1,32,1152]{3,2,0,1:T(8,128)(2,1)}, bf16[1,1,32,1152]{3,2,0,1:T(8,128)(2,1)}, u32[]{:S(2)}, u32[]{:S(2)}) collective-permute-start(bf16[1,1,32,1152]{3,2,0,1:T(8,128)(2,1)} %get-tuple-element.25), channel_id=1, source_target_pairs={{0,11},{1,12},{2,13},{3,14},{4,15},{5,0},{6,1},{7,2},{8,3},{9,4},{... | collective-permute-start | bytes 221192 | tf_op jit(solution)/shard_map/ppermute | solution.py:40
  343.9 18.1 %collective-permute-start.41 = (bf16[1,1,32,1152]{3,2,0,1:T(8,128)(2,1)}, bf16[1,1,32,1152]{3,2,0,1:T(8,128)(2,1)}, u32[]{:S(2)}, u32[]{:S(2)}) collective-permute-start(bf16[1,1,32,1152]{3,2,0,1:T(8,128)(2,1)} %get-tuple-element.24), channel_id=1, source_target_pairs={{0,12},{1,13},{2,14},{3,15},{4,0},{5,1},{6,2},{7,3},{8,4},{9,5},{1... | collective-permute-start | bytes 221192 | tf_op jit(solution)/shard_map/ppermute | solution.py:40
  344.3 18.6 %collective-permute-start.42 = (bf16[1,1,32,1152]{3,2,0,1:T(8,128)(2,1)}, bf16[1,1,32,1152]{3,2,0,1:T(8,128)(2,1)}, u32[]{:S(2)}, u32[]{:S(2)}) collective-permute-start(bf16[1,1,32,1152]{3,2,0,1:T(8,128)(2,1)} %get-tuple-element.23), channel_id=1, source_target_pairs={{0,13},{1,14},{2,15},{3,0},{4,1},{5,2},{6,3},{7,4},{8,5},{9,6},{10... | collective-permute-start | bytes 221192 | tf_op jit(solution)/shard_map/ppermute | solution.py:40
  344.4 19.5 %collective-permute-start.43 = (bf16[1,1,32,1152]{3,2,0,1:T(8,128)(2,1)}, bf16[1,1,32,1152]{3,2,0,1:T(8,128)(2,1)}, u32[]{:S(2)}, u32[]{:S(2)}) collective-permute-start(bf16[1,1,32,1152]{3,2,0,1:T(8,128)(2,1)} %get-tuple-element.22), channel_id=1, source_target_pairs={{0,14},{1,15},{2,0},{3,1},{4,2},{5,3},{6,4},{7,5},{8,6},{9,7},{10,... | collective-permute-start | bytes 221192 | tf_op jit(solution)/shard_map/ppermute | solution.py:40
  347.4 17.4 %collective-permute-start.44 = (bf16[1,1,32,1152]{3,2,0,1:T(8,128)(2,1)}, bf16[1,1,32,1152]{3,2,0,1:T(8,128)(2,1)}, u32[]{:S(2)}, u32[]{:S(2)}) collective-permute-start(bf16[1,1,32,1152]{3,2,0,1:T(8,128)(2,1)} %get-tuple-element.21), channel_id=1, source_target_pairs={{0,15},{1,0},{2,1},{3,2},{4,3},{5,4},{6,5},{7,6},{8,7},{9,8},{10,9... | collective-permute-start | bytes 221192 | tf_op jit(solution)/shard_map/ppermute | solution.py:40
  350.8 52.6 %all-to-all-start.1 = ((bf16[16,32,1152]{2,1,0:T(8,128)(2,1)}), bf16[16,32,1152]{2,1,0:T(8,128)(2,1)S(1)}, u32[]{:S(2)}, u32[]{:S(2)}) async-start(bf16[16,32,1152]{2,1,0:T(8,128)(2,1)} %gather_fusion.1), calls=%async_computation.4 | async-start | bytes 2359296 | tf_op jit(solution)/shard_map/all_to_all | solution.py:235
  404.5 33.2 %all-to-all-start.2 = ((bf16[16,32,1152]{2,1,0:T(8,128)(2,1)}), bf16[16,32,1152]{2,1,0:T(8,128)(2,1)}, u32[]{:S(2)}, u32[]{:S(2)}) async-start(bf16[16,32,1152]{2,1,0:T(8,128)(2,1)} %gather_fusion.2), calls=%async_computation.5 | async-start | bytes 2359296 | tf_op jit(solution)/shard_map/all_to_all | solution.py:235
  (68 other events, 1313.8 us)
Sparse Core Ops, SparseCore 0:
  10.1 36.2 all-gather.6
  48.6 50.9 all-gather.4
  101.8 49.0 all-gather.8
  167.2 32.7 reduce-scatter.7
  204.7 103.3 reduce-scatter.3
  312.4 89.1 reduce-scatter.5
